TPU v7x, 32 devices: a whole 2x2x4 slice. The times are simulated.
32 devices in a mesh: dp: 4 (over x, core), tm: 8 (over z, y).
Axes of the slice: x: 2, y: 2, z: 4, core: 2. Of those that a mesh axis runs over, the one named last changes fastest.
Arguments:
- latent: float32 [4, 64, 4096], P('dp', None, 'tm'), may hold values from -40 to 40
- target: float32 [4, 8192], P('dp', 'tm'), may hold values from -20 to 20
- up_kernel: float32 [4, 32, 64], replicated, may hold values from -0.5 to 0.5
- inner_kernel: float32 [3, 16, 32], replicated, may hold values from -0.625 to 0.625
- outer_kernel: float32 [32, 16], replicated, may hold values from -1.5 to 1.5
- out_kernel: float32 [7, 32], replicated, may hold values from -0.375 to 0.375
Outputs:
- latent_grad: float32 [4, 64, 4096], P('dp', None, 'tm')
- up_update: float32 [4, 32, 64], replicated
- inner_update: float32 [3, 16, 32], replicated
- outer_update: float32 [32, 16], replicated
- out_update: float32 [7, 32], replicated
All inputs are finite; a program needn't handle non-finite values.
Results may differ from a plain program's by a relative error of at most 0.0003.
Values sent between devices are 32-bit elements; how exact they have to be, the bound alone decides.
No kernel may reach another device: no remote copies, remote signals or barrier semaphores. Data moves between devices by JAX's collectives and lax.ppermute only.
A program may use at most 64 MiB of HBM per device.

v0:
```python
import jax
import jax.numpy as jnp
from jax import lax
from jax.sharding import PartitionSpec as P

MELS = 64
WIN_COARSE = 1024
WIN_FINE = 256
LOSS_WEIGHTS = (0.25, 0.5, 0.5)


def padded_2(cells, sides, width):
    for axis, dim in sides:
        count = lax.axis_size(axis)
        ends = count - 1
        head = lax.slice_in_dim(cells, 0, width, axis=dim)
        tail = lax.slice_in_dim(cells, cells.shape[dim] - width, cells.shape[dim], axis=dim)
        cells = jnp.concatenate(
            [
                lax.ppermute(tail, axis, [(i, (i + 1) % count) for i in range(ends)]),
                cells,
                lax.ppermute(head, axis, [((i + 1) % count, i) for i in range(ends)]),
            ],
            axis=dim,
        )
    return cells


def from_behind(x, axis, by):
    peers = lax.axis_size(axis)
    pairs = [(i, i + by) for i in range(peers) if 0 <= i + by < peers]
    return lax.ppermute(x, axis, pairs)


def product(form, left, right):
    return jnp.einsum(
        form, left, right, precision=lax.Precision.HIGHEST, preferred_element_type=jnp.float32
    )


def mel_bank(window, mel_count):
    half_window = window // 2
    top_mel = 2595.0 * jnp.log10(1.0 + 12000.0 / 700.0)
    points = (jnp.arange(mel_count + 1, dtype=jnp.float32) + 1.0) / (mel_count + 2.0) * top_mel
    centers = 700.0 * (jnp.power(10.0, points / 2595.0) - 1.0) / 12000.0 * half_window
    spacing = jnp.maximum(centers[1:] - centers[:-1], 1.0)
    places = jnp.arange(half_window, dtype=jnp.float32)[:, None]
    return jnp.maximum(0.0, 1.0 - jnp.abs(places - centers[None, :mel_count]) / spacing[None, :])


def dft_table(window):
    half_window = window // 2
    sample = jnp.arange(window, dtype=jnp.int32)[:, None]
    freq_index = jnp.arange(half_window, dtype=jnp.int32)[None, :]
    angles = (sample * freq_index % window).astype(jnp.float32) * (2.0 * jnp.pi / window)
    hann_taper = 0.5 - 0.5 * jnp.cos(sample.astype(jnp.float32) * (2.0 * jnp.pi / window))
    return jnp.concatenate([hann_taper * jnp.cos(angles), -hann_taper * jnp.sin(angles)], axis=1)


def framed(signal, window, frame_count):
    hop_size = window // 4
    blocks = signal.reshape(signal.shape[:-1] + (frame_count + 3, hop_size))
    return jnp.concatenate(
        [blocks[..., offset : offset + frame_count, :] for offset in range(4)], axis=-1
    )


def mel_energy(signal, window, frame_count):
    frames = framed(signal, window, frame_count)
    spectra = product("...nf,fk->...nk", frames, dft_table(window))
    half_window = window // 2
    energy = spectra[..., :half_window] ** 2 + spectra[..., half_window:] ** 2
    return product("...nk,km->...nm", energy, mel_bank(window, MELS))


def spectral_loss(signal, target_mel, window, frame_count):
    level = jnp.sqrt(mel_energy(signal, window, frame_count) + 1.0)
    return jnp.sum((level - jnp.sqrt(target_mel + 1.0)) ** 2)


def elu_slope(values):
    return jnp.where(values > 0, 1.0, jnp.exp(jnp.minimum(values, 0.0)))


def apply_mask(values, mask):
    return values * mask


def upsample_forward(values, kernel, stride, previous):
    lagged = jnp.concatenate([previous, values[:, :, :-1]], axis=2)
    phases = product("pij,bjm->bimp", kernel[:stride], values) + product(
        "pij,bjm->bimp", kernel[stride:], lagged
    )
    return (phases.reshape(phases.shape[0], phases.shape[1], -1), lagged)


def taps_forward(padded, kernel, length):
    summed = product("oi,bil->bol", kernel[0], padded[:, :, :length])
    for offset in range(1, kernel.shape[0]):
        summed = summed + product(
            "oi,bil->bol", kernel[offset], padded[:, :, offset : offset + length]
        )
    return summed


def decode_forward(activated, weights, movers, clip_mask):
    up_kernel, inner_kernel, outer_kernel, out_kernel = weights
    lend_frame, border_inner, border_output = movers
    upper, lagged = upsample_forward(activated, up_kernel, 2, lend_frame(activated[:, :, -1:]))
    upper = apply_mask(upper, clip_mask)
    padded_inner = border_inner(jax.nn.elu(upper))
    inner_out = taps_forward(padded_inner, inner_kernel, upper.shape[2])
    hidden = jax.nn.elu(inner_out)
    mixed = apply_mask(upper + product("oi,bil->bol", outer_kernel, hidden), clip_mask)
    padded_output = border_output(jax.nn.elu(mixed))
    waveform = taps_forward(padded_output, out_kernel[:, None, :], upper.shape[2])[:, 0, :]
    return (waveform, (upper, lagged, padded_inner, inner_out, hidden, mixed, padded_output))


def taps_backward(grad_out, padded, kernel, length, keep):
    tap_count = kernel.shape[0]
    row_grad = apply_mask(grad_out, keep)
    kernel_rows = jnp.stack(
        [
            product("nbol,bil->nboi", row_grad, padded[:, :, offset : offset + length])
            for offset in range(tap_count)
        ],
        axis=2,
    )
    spread = jnp.zeros(grad_out.shape[:2] + (kernel.shape[2], length + tap_count - 1), jnp.float32)
    for offset in range(tap_count):
        moved = product("oi,nbol->nbil", kernel[offset], grad_out)
        spread = spread + jnp.pad(moved, ((0, 0), (0, 0), (0, 0), (offset, tap_count - 1 - offset)))
    return (kernel_rows, spread)


def rims_backward(spread, rim_width):
    interior = spread[..., rim_width:-rim_width]
    return interior


def residual_backward(
    grad_mixed, upper, padded, inner_out, hidden, inner_kernel, outer_kernel, keep
):
    length = upper.shape[-1]
    outer_rows = product("nbol,bil->nboi", apply_mask(grad_mixed, keep), hidden)
    grad_inner = product("oi,nbol->nbil", outer_kernel, grad_mixed) * elu_slope(inner_out)
    inner_rows, spread = taps_backward(grad_inner, padded, inner_kernel, length, keep)
    grad_rectified = rims_backward(spread, 1)
    return (grad_mixed + grad_rectified * elu_slope(upper), inner_rows, outer_rows)


def upsample_backward(grad_upper, values, lagged, kernel, stride, keep):
    phase_shape = grad_upper.shape[:3] + (values.shape[-1], stride)
    grad_phase = grad_upper.reshape(phase_shape)
    row_phase = apply_mask(grad_upper, keep).reshape(phase_shape)
    first_rows = product("nbimp,bjm->nbpij", row_phase, values)
    second_rows = product("nbimp,bjm->nbpij", row_phase, lagged)
    grad_values = product("pij,nbimp->nbjm", kernel[:stride], grad_phase)
    grad_lagged = product("pij,nbimp->nbjm", kernel[stride:], grad_phase)
    arrived = jnp.zeros_like(grad_lagged[..., :1])
    grad_values = grad_values + jnp.concatenate([grad_lagged[..., 1:], arrived], axis=-1)
    return (grad_values, jnp.concatenate([first_rows, second_rows], axis=2))


def local(latent, target, up_kernel, inner_kernel, outer_kernel, out_kernel):
    weights = (up_kernel, inner_kernel, outer_kernel, out_kernel)
    clips_here = target.shape[0]
    samples = target.shape[1]
    frames_here = latent.shape[2]
    latent_in = padded_2(latent, (("tm", 2),), 4)
    start_frame = 4
    margin = 8

    def lend_frame(edge):
        return jnp.zeros_like(edge)

    def border_inner(values):
        return jnp.pad(values, ((0, 0), (0, 0), (1, 1)))

    def border_output(values):
        return jnp.pad(values, ((0, 0), (0, 0), (3, 3)))

    shard_index = lax.axis_index("tm")
    shard_total = lax.axis_size("tm")
    wide_length = samples + 2 * margin
    local_places = jnp.arange(wide_length, dtype=jnp.int32)
    clip_places = samples * shard_index - margin + local_places
    clip_mask = ((clip_places >= 0) & (clip_places < samples * shard_total)).astype(jnp.float32)
    keep_rows = ((local_places >= margin) & (local_places < margin + samples)).astype(jnp.float32)
    activated = jax.nn.elu(latent_in)
    wave_all, saved = decode_forward(
        activated, weights, (lend_frame, border_inner, border_output), clip_mask
    )
    upper, lagged, padded_inner, inner_out, hidden, mixed, padded_output = saved
    waveform = wave_all[:, margin : margin + samples]
    tail_length = 3 * WIN_COARSE // 4
    wave_next, target_next = from_behind(
        (waveform[:, :tail_length], target[:, :tail_length]), "tm", -1
    )
    long_wave = jnp.concatenate([waveform, wave_next], axis=1)
    long_target = jnp.concatenate([target, target_next], axis=1)
    gradients = [2.0 * (waveform - target)]
    tails = []
    for window in (WIN_COARSE, WIN_FINE):
        hop_size = window // 4
        frame_count = samples // hop_size
        span = samples + 3 * hop_size
        target_mel = mel_energy(long_target[:, :span], window, frame_count)

        def scale_loss(signal):
            return spectral_loss(signal, target_mel, window, frame_count)

        local_grad = jax.grad(scale_loss)(long_wave[:, :span])
        gradients.append(local_grad[:, :samples])
        tails.append(jnp.pad(local_grad[:, samples:], ((0, 0), (0, tail_length - 3 * hop_size))))
    coarse_in, fine_in = from_behind((tails[0], tails[1]), "tm", 1)
    gradients[1] = gradients[1] + jnp.pad(coarse_in, ((0, 0), (0, samples - tail_length)))
    gradients[2] = gradients[2] + jnp.pad(fine_in, ((0, 0), (0, samples - tail_length)))
    squares = jnp.stack([jnp.sum(member * member, axis=1) for member in gradients], axis=1)
    squares = lax.psum(squares, "tm")
    total_samples = samples * lax.axis_size("tm")
    grad_scale = jnp.asarray(LOSS_WEIGHTS, jnp.float32)[None, :] / jnp.sqrt(
        squares / total_samples + 1e-06
    )
    streams = (
        gradients[0] * grad_scale[:, 0, None]
        + gradients[1] * grad_scale[:, 1, None]
        + gradients[2] * grad_scale[:, 2, None]
    )[None]
    row_weights = jnp.ones((1, clips_here), jnp.float32)
    streams_wide = padded_2(streams, (("tm", 2),), 8)
    wave_length = mixed.shape[2]
    out_taps = out_kernel[:, None, :]
    kernel_rows_out, spread_out = taps_backward(
        streams_wide[:, :, None, :], padded_output, out_taps, wave_length, keep_rows
    )
    out_rows = kernel_rows_out[:, :, :, 0, :]
    grad_final = rims_backward(spread_out, 3)
    grad_mixed = apply_mask(grad_final * elu_slope(mixed), clip_mask)
    grad_upper, inner_rows, outer_rows = residual_backward(
        grad_mixed, upper, padded_inner, inner_out, hidden, inner_kernel, outer_kernel, keep_rows
    )
    grad_activated, up_rows = upsample_backward(
        apply_mask(grad_upper, clip_mask), activated, lagged, up_kernel, 2, keep_rows
    )
    grad_latent_rows = grad_activated[..., start_frame : start_frame + frames_here] * elu_slope(
        latent
    )
    latent_grad = product("nb,nbcm->bcm", row_weights, grad_latent_rows)
    local_totals = [
        product("nb,nb...->...", row_weights, member)
        for member in (up_rows, inner_rows, outer_rows, out_rows)
    ]
    param_count = sum((member.size for member in local_totals))
    summed = lax.psum(
        (local_totals[0], local_totals[1], local_totals[2], local_totals[3]), ("dp", "tm")
    )
    squares_all = sum((jnp.sum(member * member) for member in summed))
    factor = jnp.minimum(1.0, 1.0 / jnp.sqrt(squares_all / param_count + 1e-06))
    updates = [member * factor for member in summed]
    return (latent_grad, updates[0], updates[1], updates[2], updates[3])


def solution(mesh):
    placed = (P("dp", None, "tm"), P("dp", "tm"), P(), P(), P(), P())
    return jax.shard_map(
        local,
        mesh=mesh,
        in_specs=placed,
        out_specs=(P("dp", None, "tm"), P(), P(), P(), P()),
        check_vma=False,
    )
```

profile of v0, /device:TPU:0, one launch (start us, length us, event | category | flops | bytes accessed | tf_op | source)
XLA Modules:
  0.0 188.2 jit_solution(7671481007626582187)
XLA Ops:
  0.6 1.3 slice.296
  1.9 1.3 collective-permute-start.3
  4.1 5.5 %collective-permute-start = (f32[1,64,4]{2,1,0:T(8,128)S(1)}, f32[1,64,4]{2,1,0:T(8,128)S(1)}, u32[]{:S(2)}, u32[]{:S(2)}) collective-permute-start(f32[1,64,4]{2,1,0:T(8,128)S(1)} %get-tuple-element.15), channel_id=1, source_target_pairs={{0,1},{1,2},{2,3},{3,4},{4,5},{5,6},{6,7},{8,9},{9,10},{10,11},{11... | collective-permute-start | bytes 3080 | tf_op jit(solution)/shard_map/ppermute | solution.py:20
  9.6 1.3 collective-permute-start.1
  12.3 1.6 slice_bitcast_fusion.6
  13.9 1.2 sine_multiply_fusion.1
  15.1 9.4 %sine_multiply_fusion = (f32[1024,512]{1,0:T(8,128)S(1)}, f32[1024,512]{1,0:T(8,128)}) fusion(f32[1024]{0:T(1024)S(1)} %fusion.218, f32[1024]{0:T(1024)S(1)} %multiply_subtract_fusion), kind=kLoop, calls=%fused_computation.21 | loop fusion | flops 8388608 | bytes 4202496 | tf_op jit(solution)/shard_map/jvp()/mul | solution.py:57
  25.3 1.1 compare_select_fusion
  26.7 1.2 copy.16
  28.1 1.0 fusion.69
  29.1 1.3 convolution_add_fusion.1
  30.4 1.0 fusion.5
  31.4 1.3 compare_select_fusion.9
  32.7 1.0 convolution_reduce_fusion.2
  33.7 1.0 convolution_reduce_fusion.1
  34.7 1.0 convolution_reduce_fusion
  35.7 1.0 convolution_reduce_fusion.5
  36.7 1.0 convolution_reduce_fusion.4
  37.6 1.0 convolution_reduce_fusion.6
  38.6 1.0 convolution_reduce_fusion.3
  39.6 2.0 %multiply_reduce_fusion.6 = (f32[]{:T(128)}, f32[1,1024]{1,0:T(1,128)}, f32[1,1792]{1,0:T(1,128)S(1)}) fusion(f32[1,1024]{1,0:T(1,128)} %param.8, f32[1,1040]{1,0:T(1,128)S(1)} %squeeze.11), kind=kLoop, calls=%fused_computation.340 | loop fusion | flops 4094 | bytes 16388 | tf_op jit(solution)/shard_map/reduce_sum | solution.py:220
  42.3 1.3 collective-permute-start.2
  45.4 1.3 reduce.11
  46.7 1.3 reshape.962
  48.0 1.4 reshape.970
  51.1 4.3 %fusion.15 = f32[1,4,1024]{2,1,0:T(4,128)} fusion(f32[1024,512]{1,0:T(8,128)S(1)} %get-tuple-element.77, f32[1024,512]{1,0:T(8,128)} %get-tuple-element.78, f32[1,4,256]{2,1,0:T(4,128)S(1)} %get-tuple-element.45, f32[1,4,256]{2,1,0:T(4,128)S(1)} %get-tuple-element.46, f32[1,4,256]{2,1,0:T(4,128)S(1)} %get-tuple-element.47, ...), kind=kOutput, calls=%fused_computation.33 | convolution fusion | flops 51392512 | bytes 4227072 | tf_op jit(solution)/shard_map/...nf,fk->...nk/dot_general | solution.py:36
  55.4 0.9 convolution_bitcast_fusion.10
  56.3 1.3 maximum_reduce_fusion
  57.6 1.3 reshape.959
  58.9 1.3 fusion.210
  60.2 1.4 reshape.967
  61.6 1.4 fusion.285
  63.0 0.9 fusion.283
  63.9 1.2 convolution_bitcast_fusion.11
  65.9 0.9 fusion.20
  67.6 1.3 convolution_bitcast_fusion.9
  69.7 1.4 reshape.974
  71.7 6.2 %collective-permute-start.5 = (f32[1,768]{1,0:T(1,128)S(1)}, f32[1,768]{1,0:T(1,128)S(1)}, u32[]{:S(2)}, u32[]{:S(2)}) collective-permute-start(f32[1,768]{1,0:T(1,128)S(1)} %pad.112), channel_id=1, source_target_pairs={{0,1},{1,2},{2,3},{3,4},{4,5},{5,6},{6,7},{8,9},{9,10},{10,11},{11... | collective-permute-start | bytes 9224 | tf_op jit(solution)/shard_map/ppermute | solution.py:32
  78.0 3.7 %fusion.14 = f32[1,4,1024]{2,1,0:T(4,128)S(1)} fusion(f32[1024,512]{1,0:T(8,128)S(1)} %get-tuple-element.77, f32[1024,512]{1,0:T(8,128)} %get-tuple-element.78, f32[1,4,256]{2,1,0:T(4,128)} %get-tuple-element.49, f32[1,4,256]{2,1,0:T(4,128)} %get-tuple-element.50, f32[1,4,256]{2,1,0:T(4,128)} %get-tuple-element.51, f32[1,4,256]{2,1,0:T(4,128)} %get-tuple-element.48), kind=kOutput, calls=%fused_computation.32 | convolution fusion | flops 51392512 | bytes 4227072 | tf_op jit(solution)/shard_map/jvp(...nf,fk->...nk)/dot_general | solution.py:36
  83.3 3.5 %fusion.16 = f32[1,4,1024]{2,1,0:T(4,128)S(1)} fusion(f32[1024,512]{1,0:T(8,128)S(1)} %get-tuple-element.77, f32[1024,512]{1,0:T(8,128)S(1)} %copy-done.1, f32[1,4,512]{2,1,0:T(4,128)S(1)} %get-tuple-element.18, f32[1,4,512]{2,1,0:T(4,128)S(1)} %get-tuple-element.17), kind=kOutput, calls=%fused_computation.34 | convolution fusion | flops 51384320 | bytes 4227072 | tf_op jit(solution)/shard_map/transpose(jvp(...nf,fk->...nk))/dot_general | solution.py:36
  86.9 5.0 %collective-permute-start.4 = (f32[1,768]{1,0:T(1,128)S(1)}, f32[1,768]{1,0:T(1,128)S(1)}, u32[]{:S(2)}, u32[]{:S(2)}) collective-permute-start(f32[1,768]{1,0:T(1,128)S(1)} %slice.347), channel_id=1, source_target_pairs={{0,1},{1,2},{2,3},{3,4},{4,5},{5,6},{6,7},{8,9},{9,10},{10,11},{11... | collective-permute-start | bytes 9224 | tf_op jit(solution)/shard_map/ppermute | solution.py:32
  93.8 2.0 %pad_maximum_fusion.16 = f32[1,3]{1,0:T(1,128)S(1)} fusion(f32[1,1]{1,0:T(1,128)} %bitcast.63, f32[1,1]{1,0:T(1,128)} %bitcast.53, f32[1,1]{1,0:T(1,128)} %bitcast.43), kind=kLoop, calls=%fused_computation.344 | loop fusion | flops 6 | bytes 24 | tf_op jit(solution)/shard_map/stack | solution.py:220
  96.0 22.0 %psum.35 = f32[1,3]{1,0:T(1,128)S(1)} all-reduce(f32[1,3]{1,0:T(1,128)S(1)} %pad_maximum_fusion.16), channel_id=1, replica_groups=mesh['dp'=4,'tm'=8] {'tm'}, use_global_device_ids=true, to_apply=%region_3.4 | all-reduce | flops 3 | bytes 24 | tf_op jit(solution)/shard_map/psum | solution.py:221
  119.8 2.1 %add_bitcast_fusion.1 = f32[1,1,1024]{2,1,0:T(1,128)S(1)} fusion(f32[1,1024]{1,0:T(1,128)S(1)} %get-tuple-element.14, f32[1,1024]{1,0:T(1,128)S(1)} %get-tuple-element.12, f32[]{:T(128)} %bitcast.66, f32[]{:T(128)} %bitcast.65, f32[]{:T(128)} %bitcast.64, f32[1,1024]{1,0:T(1,128)} %param.8, f32[1,1040]{1,0:T(1,128)} %copy-done.14), kind=kLoop, calls=%fused_computation.336 | loop fusion | flops 6144 | bytes 20492 | tf_op jit(solution)/shard_map/broadcast_in_dim | solution.py:226
  122.0 1.3 collective-permute-start.7
  123.3 4.5 %collective-permute-start.6 = (f32[1,1,8]{2,1,0:T(1,128)S(1)}, f32[1,1,8]{2,1,0:T(1,128)S(1)}, u32[]{:S(2)}, u32[]{:S(2)}) collective-permute-start(f32[1,1,8]{2,1,0:T(1,128)S(1)} %get-tuple-element.62), channel_id=1, source_target_pairs={{0,1},{1,2},{2,3},{3,4},{4,5},{5,6},{6,7},{8,9},{9,10},{10,11},{11... | collective-permute-start | bytes 104 | tf_op jit(solution)/shard_map/ppermute | solution.py:20
  127.8 1.3 collective-permute-done.6
  136.8 41.8 %all-reduce.29 = (f32[4,32,64]{2,1,0:T(8,128)S(1)}, f32[3,16,32]{2,1,0:T(8,128)S(1)}, f32[32,16]{0,1:T(8,128)S(1)}, f32[7,32]{1,0:T(8,128)S(1)}) all-reduce(f32[4,32,64]{2,1,0:T(8,128)S(1)} %maximum_bitcast_fusion, f32[3,16,32]{2,1,0:T(8,128)S(1)} %maximum_bitcast_fusion.1, ...), channel_id=1, replica_groups=mesh['dp'=4,'tm'=8] {'dp','tm'}, use_global_device_ids=true, to_apply=%region_4.5 | all-reduce | flops 10464 | bytes 83712 | tf_op jit(solution)/shard_map/psum | solution.py:256
  (141 shorter events, 30.2 us)
Async XLA Ops:
  0.6 30.8 %copy-start = (f32[32,16]{0,1:T(8,128)S(1)}, f32[32,16]{0,1:T(8,128)}, u32[]{:S(2)}) copy-start(f32[32,16]{0,1:T(8,128)} %param.11) | copy-start | bytes 6148
  1.9 41.6 %collective-permute-start.3 = (f32[1,768]{1,0:T(1,128)}, f32[1,768]{1,0:T(1,128)}, u32[]{:S(2)}, u32[]{:S(2)}) collective-permute-start(f32[1,768]{1,0:T(1,128)} %slice.296), channel_id=1, source_target_pairs={{1,0},{2,1},{3,2},{4,3},{5,4},{6,5},{7,6},{9,8},{10,9},{11,10},{12... | collective-permute-start | bytes 9224 | tf_op jit(solution)/shard_map/ppermute | solution.py:32
  4.1 20.5 %collective-permute-start = (f32[1,64,4]{2,1,0:T(8,128)S(1)}, f32[1,64,4]{2,1,0:T(8,128)S(1)}, u32[]{:S(2)}, u32[]{:S(2)}) collective-permute-start(f32[1,64,4]{2,1,0:T(8,128)S(1)} %get-tuple-element.15), channel_id=1, source_target_pairs={{0,1},{1,2},{2,3},{3,4},{4,5},{5,6},{6,7},{8,9},{9,10},{10,11},{11... | collective-permute-start | bytes 3080 | tf_op jit(solution)/shard_map/ppermute | solution.py:20
  9.6 15.0 %collective-permute-start.1 = (f32[1,64,4]{2,1,0:T(8,128)S(1)}, f32[1,64,4]{2,1,0:T(8,128)S(1)}, u32[]{:S(2)}, u32[]{:S(2)}) collective-permute-start(f32[1,64,4]{2,1,0:T(8,128)S(1)} %get-tuple-element.16), channel_id=1, source_target_pairs={{1,0},{2,1},{3,2},{4,3},{5,4},{6,5},{7,6},{9,8},{10,9},{11,10},{12... | collective-permute-start | bytes 3080 | tf_op jit(solution)/shard_map/ppermute | solution.py:22
  15.1 9.5 %copy-start.7 = (f32[1,64,512]{2,1,0:T(8,128)S(1)}, f32[1,64,512]{2,1,0:T(8,128)}, u32[]{:S(2)}) copy-start(f32[1,64,512]{2,1,0:T(8,128)} %param.7) | copy-start | bytes 393220
  15.1 9.5 %copy-start.11 = (f32[4,32,64]{2,1,0:T(8,128)S(1)}, f32[4,32,64]{2,1,0:T(8,128)}, u32[]{:S(2)}) copy-start(f32[4,32,64]{2,1,0:T(8,128)} %param.9) | copy-start | bytes 98308
  24.6 0.6 copy-start.17
  24.6 0.6 copy-start.19
  25.3 1.1 copy-start.4
  28.0 2.4 %copy-start.6 = (f32[1,32,1040]{2,1,0:T(8,128)}, f32[1,32,1040]{2,1,0:T(8,128)S(1)}, u32[]{:S(2)}) copy-start(f32[1,32,1040]{2,1,0:T(8,128)S(1)} %copy.17) | copy-start | bytes 399364
  32.7 5.9 %copy-start.9 = (f32[1,32,1040]{2,1,0:T(8,128)}, f32[1,32,1040]{2,1,0:T(8,128)S(1)}, u32[]{:S(2)}) copy-start(f32[1,32,1040]{2,1,0:T(8,128)S(1)} %get-tuple-element.74) | copy-start | bytes 399364
  39.6 2.0 %copy-start.14 = (f32[1,1040]{1,0:T(1,128)}, f32[1,1040]{1,0:T(1,128)S(1)}, u32[]{:S(2)}) copy-start(f32[1,1040]{1,0:T(1,128)S(1)} %squeeze.11) | copy-start | bytes 12484
  42.3 14.1 %collective-permute-start.2 = (f32[1,768]{1,0:T(1,128)}, f32[1,768]{1,0:T(1,128)}, u32[]{:S(2)}, u32[]{:S(2)}) collective-permute-start(f32[1,768]{1,0:T(1,128)} %slice.333), channel_id=1, source_target_pairs={{1,0},{2,1},{3,2},{4,3},{5,4},{6,5},{7,6},{9,8},{10,9},{11,10},{12... | collective-permute-start | bytes 9224 | tf_op jit(solution)/shard_map/ppermute | solution.py:32
  44.2 0.6 copy-start.15
  51.1 4.3 %copy-start.2 = (f32[256,128]{1,0:T(8,128)S(1)}, f32[256,128]{1,0:T(8,128)}, u32[]{:S(2)}) copy-start(f32[256,128]{1,0:T(8,128)} %get-tuple-element.75) | copy-start | bytes 393220
  51.1 4.3 %copy-start.3 = (f32[256,128]{1,0:T(8,128)S(1)}, f32[256,128]{1,0:T(8,128)}, u32[]{:S(2)}) copy-start(f32[256,128]{1,0:T(8,128)} %get-tuple-element.76) | copy-start | bytes 393220
  51.1 5.2 %copy-start.16 = (f32[1,1024]{1,0:T(1,128)S(1)}, f32[1,1024]{1,0:T(1,128)}, u32[]{:S(2)}) copy-start(f32[1,1024]{1,0:T(1,128)} %get-tuple-element.53) | copy-start | bytes 12292
  71.7 20.1 %collective-permute-start.5 = (f32[1,768]{1,0:T(1,128)S(1)}, f32[1,768]{1,0:T(1,128)S(1)}, u32[]{:S(2)}, u32[]{:S(2)}) collective-permute-start(f32[1,768]{1,0:T(1,128)S(1)} %pad.112), channel_id=1, source_target_pairs={{0,1},{1,2},{2,3},{3,4},{4,5},{5,6},{6,7},{8,9},{9,10},{10,11},{11... | collective-permute-start | bytes 9224 | tf_op jit(solution)/shard_map/ppermute | solution.py:32
  78.0 3.7 %copy-start.23 = (f32[64]{0:T(128)S(1)}, f32[64]{0:T(128)}, u32[]{:S(2)}) copy-start(f32[64]{0:T(128)} %get-tuple-element.67) | copy-start | bytes 772
  78.0 3.7 %copy-start.24 = (f32[64]{0:T(128)S(1)}, f32[64]{0:T(128)}, u32[]{:S(2)}) copy-start(f32[64]{0:T(128)} %get-tuple-element.68) | copy-start | bytes 772
  78.0 4.1 %copy-start.22 = (f32[1,4,1024]{2,1,0:T(4,128)S(1)}, f32[1,4,1024]{2,1,0:T(4,128)}, u32[]{:S(2)}) copy-start(f32[1,4,1024]{2,1,0:T(4,128)} %fusion.15) | copy-start | bytes 49156
  81.7 1.6 copy-start.1
  83.3 8.6 %copy-start.21 = (f32[1,1216]{1,0:T(1,128)S(1)}, f32[1,1216]{1,0:T(1,128)}, u32[]{:S(2)}) copy-start(f32[1,1216]{1,0:T(1,128)} %reshape.974) | copy-start | bytes 14596
  86.8 43.6 %copy-start.10 = (f32[1,32,1040]{2,1,0:T(8,128)S(1)}, f32[1,32,1040]{2,1,0:T(8,128)}, u32[]{:S(2)}) copy-start(f32[1,32,1040]{2,1,0:T(8,128)} %copy-done.9) | copy-start | bytes 399364
  86.9 6.3 %collective-permute-start.4 = (f32[1,768]{1,0:T(1,128)S(1)}, f32[1,768]{1,0:T(1,128)S(1)}, u32[]{:S(2)}, u32[]{:S(2)}) collective-permute-start(f32[1,768]{1,0:T(1,128)S(1)} %slice.347), channel_id=1, source_target_pairs={{0,1},{1,2},{2,3},{3,4},{4,5},{5,6},{6,7},{8,9},{9,10},{10,11},{11... | collective-permute-start | bytes 9224 | tf_op jit(solution)/shard_map/ppermute | solution.py:32
  122.0 5.8 %collective-permute-start.7 = (f32[1,1,8]{2,1,0:T(1,128)S(1)}, f32[1,1,8]{2,1,0:T(1,128)S(1)}, u32[]{:S(2)}, u32[]{:S(2)}) collective-permute-start(f32[1,1,8]{2,1,0:T(1,128)S(1)} %get-tuple-element.61), channel_id=1, source_target_pairs={{1,0},{2,1},{3,2},{4,3},{5,4},{6,5},{7,6},{9,8},{10,9},{11,10},{12... | collective-permute-start | bytes 104 | tf_op jit(solution)/shard_map/ppermute | solution.py:22
  123.3 5.8 %collective-permute-start.6 = (f32[1,1,8]{2,1,0:T(1,128)S(1)}, f32[1,1,8]{2,1,0:T(1,128)S(1)}, u32[]{:S(2)}, u32[]{:S(2)}) collective-permute-start(f32[1,1,8]{2,1,0:T(1,128)S(1)} %get-tuple-element.62), channel_id=1, source_target_pairs={{0,1},{1,2},{2,3},{3,4},{4,5},{5,6},{6,7},{8,9},{9,10},{10,11},{11... | collective-permute-start | bytes 104 | tf_op jit(solution)/shard_map/ppermute | solution.py:20
  129.2 3.1 %copy-start.13 = (f32[3,16,32]{2,1,0:T(8,128)S(1)}, f32[3,16,32]{2,1,0:T(8,128)}, u32[]{:S(2)}) copy-start(f32[3,16,32]{2,1,0:T(8,128)} %param.10) | copy-start | bytes 18436
  131.2 2.7 %copy-start.5 = (f32[1,64,519]{2,1,0:T(8,128)S(1)}, f32[1,64,519]{2,1,0:T(8,128)}, u32[]{:S(2)}) copy-start(f32[1,64,519]{2,1,0:T(8,128)} %copy-done.4) | copy-start | bytes 398596
  131.7 2.7 %copy-start.8 = (f32[1,64,512]{2,1,0:T(8,128)S(1)}, f32[1,64,512]{2,1,0:T(8,128)}, u32[]{:S(2)}) copy-start(f32[1,64,512]{2,1,0:T(8,128)} %param.7) | copy-start | bytes 393220
  131.7 2.7 %copy-start.18 = (f32[1,64,4]{2,1,0:T(8,128)S(1)}, f32[1,64,4]{2,1,0:T(8,128)}, u32[]{:S(2)}) copy-start(f32[1,64,4]{2,1,0:T(8,128)} %copy-done.17) | copy-start | bytes 3076
  131.7 2.7 %copy-start.20 = (f32[1,64,4]{2,1,0:T(8,128)S(1)}, f32[1,64,4]{2,1,0:T(8,128)}, u32[]{:S(2)}) copy-start(f32[1,64,4]{2,1,0:T(8,128)} %copy-done.19) | copy-start | bytes 3076
  134.0 52.6 %copy-start.12 = (f32[4,32,64]{2,1,0:T(8,128)S(1)}, f32[4,32,64]{2,1,0:T(8,128)}, u32[]{:S(2)}) copy-start(f32[4,32,64]{2,1,0:T(8,128)} %param.9) | copy-start | bytes 98308
where the time goes:
time: 190 us; the launch traced here: 188 us
  blocking collectives  63.8 us (34%)
  matrix products  37.6 us (20%)
  other arithmetic  31.8 us (17%)
  starting transfers between devices  26.4 us (14%)
  local copies, waits for them, and re-layouts  22 us (12%)
  between operations  4.65 us (2%)
  waiting for transfers between devices  1.95 us (1%)
    psum x1, blocking collectives, local(): lax.psum((local_totals[0], local_totals[1], local_totals[2], local_totals...  41.8 us
    dot_general x44, matrix products, product(): jnp.einsum(form, left, right, precision=lax.Precision.HIGHEST, preferred_...  37.6 us
    psum x1, blocking collectives, local(): squares = lax.psum(squares, 'tm')  22 us
    ppermute x4, starting transfers between devices, from_behind(): return lax.ppermute(x, axis, pairs)  13.8 us
    mul x2, other arithmetic, dft_table(): -hann_taper * jnp.sin(angles)  10.7 us
    ppermute x2, starting transfers between devices, padded_2(): lax.ppermute(tail, axis, [(i, (i + 1) % count) for i in range(ends)])  10.1 us
    reshape x5, local copies, waits for them, and re-layouts, framed(): blocks = signal.reshape(signal.shape[:-1] + (frame_count + 3, hop_size))  6.68 us
    slice x4, local copies, waits for them, and re-layouts, framed(): blocks[..., offset:offset + frame_count, :]  4.01 us
  transfers between devices with their start and end apart: 8, of which 2 were waited for; matrix products, arithmetic and copies ran while one was open for 28% of the time, Pallas kernels for 0%

commit v1 on v0

--- a/solution.py
+++ b/solution.py
@@ -253,9 +253,8 @@
         for member in (up_rows, inner_rows, outer_rows, out_rows)
     ]
     param_count = sum((member.size for member in local_totals))
-    summed = lax.psum(
-        (local_totals[0], local_totals[1], local_totals[2], local_totals[3]), ("dp", "tm")
-    )
+    name_keys = lambda inputs: lax.psum(lax.psum(inputs, axis_name="tm"), axis_name="dp")
+    summed = name_keys((local_totals[0], local_totals[1], local_totals[2], local_totals[3]))
     squares_all = sum((jnp.sum(member * member) for member in summed))
     factor = jnp.minimum(1.0, 1.0 / jnp.sqrt(squares_all / param_count + 1e-06))
     updates = [member * factor for member in summed]

time: 190 us -> 196 us (1.032)
  blocking collectives: 63.8 us -> 69.7 us
    psum x1 -> x2, blocking collectives: 41.8 us -> 47.8 us  [the longest x1 36.4 us: local(): lax.psum(inputs, axis_name='tm')]
  transfers between devices with their start and end apart: 8 -> 8, of which waited for: 2 -> 2; matrix products, arithmetic and copies ran while one was open for 28% -> 27% of each run, Pallas kernels for 0% -> 0%
where the time goes in v1:
time: 196 us; the launch traced here: 194 us
  blocking collectives  69.7 us (36%)
  matrix products  37.6 us (19%)
  other arithmetic  31.8 us (16%)
  starting transfers between devices  26.4 us (13%)
  local copies, waits for them, and re-layouts  21.8 us (11%)
  between operations  4.69 us (2%)
    dot_general x44, matrix products, product(): jnp.einsum(form, left, right, precision=lax.Precision.HIGHEST, preferred_...  37.6 us
    psum x1, blocking collectives, local(): lax.psum(inputs, axis_name='tm')  36.4 us
    psum x1, blocking collectives, local(): squares = lax.psum(squares, 'tm')  22 us
    ppermute x4, starting transfers between devices, from_behind(): return lax.ppermute(x, axis, pairs)  13.8 us
    psum x1, blocking collectives, local(): lax.psum(lax.psum(inputs, axis_name='tm'), axis_name='dp')  11.3 us
    mul x2, other arithmetic, dft_table(): -hann_taper * jnp.sin(angles)  10.7 us
    ppermute x2, starting transfers between devices, padded_2(): lax.ppermute(tail, axis, [(i, (i + 1) % count) for i in range(ends)])  10.1 us
    reshape x5, local copies, waits for them, and re-layouts, framed(): blocks = signal.reshape(signal.shape[:-1] + (frame_count + 3, hop_size))  6.68 us
  transfers between devices with their start and end apart: 8, of which 2 were waited for; matrix products, arithmetic and copies ran while one was open for 27% of the time, Pallas kernels for 0%

profile of v1, /device:TPU:0, one launch (start us, length us, event | category | flops | bytes accessed | tf_op | source)
XLA Modules:
  0.0 194.0 jit_solution(15026343945941691035)
XLA Ops:
  0.6 1.3 slice.296
  1.9 1.3 collective-permute-start.3
  4.1 5.5 %collective-permute-start = (f32[1,64,4]{2,1,0:T(8,128)S(1)}, f32[1,64,4]{2,1,0:T(8,128)S(1)}, u32[]{:S(2)}, u32[]{:S(2)}) collective-permute-start(f32[1,64,4]{2,1,0:T(8,128)S(1)} %get-tuple-element.19), channel_id=1, source_target_pairs={{0,1},{1,2},{2,3},{3,4},{4,5},{5,6},{6,7},{8,9},{9,10},{10,11},{11... | collective-permute-start | bytes 3080 | tf_op jit(solution)/shard_map/ppermute | solution.py:20
  9.6 1.3 collective-permute-start.1
  12.3 1.6 slice_bitcast_fusion.6
  13.9 1.2 sine_multiply_fusion.1
  15.1 9.4 %sine_multiply_fusion = (f32[1024,512]{1,0:T(8,128)S(1)}, f32[1024,512]{1,0:T(8,128)}) fusion(f32[1024]{0:T(1024)S(1)} %fusion.218, f32[1024]{0:T(1024)S(1)} %multiply_subtract_fusion), kind=kLoop, calls=%fused_computation.21 | loop fusion | flops 8388608 | bytes 4202496 | tf_op jit(solution)/shard_map/jvp()/mul | solution.py:57
  25.2 1.1 compare_select_fusion
  26.5 1.2 copy.16
  28.0 1.0 fusion.69
  29.0 1.3 convolution_add_fusion.1
  30.3 1.0 fusion.5
  31.3 1.3 compare_select_fusion.9
  32.6 1.0 convolution_reduce_fusion.2
  33.6 1.0 convolution_reduce_fusion.1
  34.6 1.0 convolution_reduce_fusion
  35.5 1.0 convolution_reduce_fusion.5
  36.5 1.0 convolution_reduce_fusion.4
  37.5 1.0 convolution_reduce_fusion.6
  38.5 1.0 convolution_reduce_fusion.3
  39.5 2.0 %multiply_reduce_fusion.6 = (f32[]{:T(128)}, f32[1,1024]{1,0:T(1,128)}, f32[1,1792]{1,0:T(1,128)S(1)}) fusion(f32[1,1024]{1,0:T(1,128)} %param.8, f32[1,1040]{1,0:T(1,128)S(1)} %squeeze.11), kind=kLoop, calls=%fused_computation.340 | loop fusion | flops 4094 | bytes 16388 | tf_op jit(solution)/shard_map/reduce_sum | solution.py:220
  42.1 1.3 collective-permute-start.2
  45.3 1.3 reduce.11
  46.6 1.3 reshape.962
  47.9 1.4 reshape.970
  51.0 4.3 %fusion.15 = f32[1,4,1024]{2,1,0:T(4,128)} fusion(f32[1024,512]{1,0:T(8,128)S(1)} %get-tuple-element.81, f32[1024,512]{1,0:T(8,128)} %get-tuple-element.82, f32[1,4,256]{2,1,0:T(4,128)S(1)} %get-tuple-element.49, f32[1,4,256]{2,1,0:T(4,128)S(1)} %get-tuple-element.50, f32[1,4,256]{2,1,0:T(4,128)S(1)} %get-tuple-element.51, ...), kind=kOutput, calls=%fused_computation.33 | convolution fusion | flops 51392512 | bytes 4227072 | tf_op jit(solution)/shard_map/...nf,fk->...nk/dot_general | solution.py:36
  55.3 0.9 convolution_bitcast_fusion.10
  56.2 1.3 maximum_reduce_fusion
  57.5 1.3 reshape.959
  58.8 1.3 fusion.210
  60.1 1.4 reshape.967
  61.4 1.4 fusion.285
  63.7 1.2 convolution_bitcast_fusion.11
  65.8 0.9 fusion.20
  67.5 1.3 convolution_bitcast_fusion.9
  69.5 1.4 reshape.974
  71.6 6.3 %collective-permute-start.5 = (f32[1,768]{1,0:T(1,128)S(1)}, f32[1,768]{1,0:T(1,128)S(1)}, u32[]{:S(2)}, u32[]{:S(2)}) collective-permute-start(f32[1,768]{1,0:T(1,128)S(1)} %pad.112), channel_id=1, source_target_pairs={{0,1},{1,2},{2,3},{3,4},{4,5},{5,6},{6,7},{8,9},{9,10},{10,11},{11... | collective-permute-start | bytes 9224 | tf_op jit(solution)/shard_map/ppermute | solution.py:32
  77.9 3.7 %fusion.14 = f32[1,4,1024]{2,1,0:T(4,128)S(1)} fusion(f32[1024,512]{1,0:T(8,128)S(1)} %get-tuple-element.81, f32[1024,512]{1,0:T(8,128)} %get-tuple-element.82, f32[1,4,256]{2,1,0:T(4,128)} %get-tuple-element.53, f32[1,4,256]{2,1,0:T(4,128)} %get-tuple-element.54, f32[1,4,256]{2,1,0:T(4,128)} %get-tuple-element.55, f32[1,4,256]{2,1,0:T(4,128)} %get-tuple-element.52), kind=kOutput, calls=%fused_computation.32 | convolution fusion | flops 51392512 | bytes 4227072 | tf_op jit(solution)/shard_map/jvp(...nf,fk->...nk)/dot_general | solution.py:36
  83.2 3.5 %fusion.16 = f32[1,4,1024]{2,1,0:T(4,128)S(1)} fusion(f32[1024,512]{1,0:T(8,128)S(1)} %get-tuple-element.81, f32[1024,512]{1,0:T(8,128)S(1)} %copy-done.1, f32[1,4,512]{2,1,0:T(4,128)S(1)} %get-tuple-element.22, f32[1,4,512]{2,1,0:T(4,128)S(1)} %get-tuple-element.21), kind=kOutput, calls=%fused_computation.34 | convolution fusion | flops 51384320 | bytes 4227072 | tf_op jit(solution)/shard_map/transpose(jvp(...nf,fk->...nk))/dot_general | solution.py:36
  86.8 5.0 %collective-permute-start.4 = (f32[1,768]{1,0:T(1,128)S(1)}, f32[1,768]{1,0:T(1,128)S(1)}, u32[]{:S(2)}, u32[]{:S(2)}) collective-permute-start(f32[1,768]{1,0:T(1,128)S(1)} %slice.347), channel_id=1, source_target_pairs={{0,1},{1,2},{2,3},{3,4},{4,5},{5,6},{6,7},{8,9},{9,10},{10,11},{11... | collective-permute-start | bytes 9224 | tf_op jit(solution)/shard_map/ppermute | solution.py:32
  93.7 2.0 %pad_maximum_fusion.16 = f32[1,3]{1,0:T(1,128)S(1)} fusion(f32[1,1]{1,0:T(1,128)} %bitcast.63, f32[1,1]{1,0:T(1,128)} %bitcast.53, f32[1,1]{1,0:T(1,128)} %bitcast.43), kind=kLoop, calls=%fused_computation.344 | loop fusion | flops 6 | bytes 24 | tf_op jit(solution)/shard_map/stack | solution.py:220
  95.8 22.0 %psum.63 = f32[1,3]{1,0:T(1,128)S(1)} all-reduce(f32[1,3]{1,0:T(1,128)S(1)} %pad_maximum_fusion.16), channel_id=1, replica_groups=mesh['dp'=4,'tm'=8] {'tm'}, use_global_device_ids=true, to_apply=%region_3.4 | all-reduce | flops 3 | bytes 24 | tf_op jit(solution)/shard_map/psum | solution.py:221
  119.7 2.1 %add_bitcast_fusion.1 = f32[1,1,1024]{2,1,0:T(1,128)S(1)} fusion(f32[1,1024]{1,0:T(1,128)S(1)} %get-tuple-element.18, f32[1,1024]{1,0:T(1,128)S(1)} %get-tuple-element.16, f32[]{:T(128)} %bitcast.66, f32[]{:T(128)} %bitcast.65, f32[]{:T(128)} %bitcast.64, f32[1,1024]{1,0:T(1,128)} %param.8, f32[1,1040]{1,0:T(1,128)} %copy-done.14), kind=kLoop, calls=%fused_computation.336 | loop fusion | flops 6144 | bytes 20492 | tf_op jit(solution)/shard_map/broadcast_in_dim | solution.py:226
  121.9 1.3 collective-permute-start.7
  123.2 4.5 %collective-permute-start.6 = (f32[1,1,8]{2,1,0:T(1,128)S(1)}, f32[1,1,8]{2,1,0:T(1,128)S(1)}, u32[]{:S(2)}, u32[]{:S(2)}) collective-permute-start(f32[1,1,8]{2,1,0:T(1,128)S(1)} %get-tuple-element.66), channel_id=1, source_target_pairs={{0,1},{1,2},{2,3},{3,4},{4,5},{5,6},{6,7},{8,9},{9,10},{10,11},{11... | collective-permute-start | bytes 104 | tf_op jit(solution)/shard_map/ppermute | solution.py:20
  127.7 1.3 collective-permute-done.6
  136.7 36.4 %all-reduce.29 = (f32[4,32,64]{2,1,0:T(8,128)S(1)}, f32[3,16,32]{2,1,0:T(8,128)S(1)}, f32[32,16]{0,1:T(8,128)S(1)}, f32[7,32]{1,0:T(8,128)S(1)}) all-reduce(f32[4,32,64]{2,1,0:T(8,128)S(1)} %maximum_bitcast_fusion, f32[3,16,32]{2,1,0:T(8,128)S(1)} %maximum_bitcast_fusion.1, ...), channel_id=1, replica_groups=mesh['dp'=4,'tm'=8] {'tm'}, use_global_device_ids=true, to_apply=%region_4.5 | all-reduce | flops 10464 | bytes 83712 | tf_op jit(solution)/shard_map/psum | solution.py:256
  173.1 11.3 %all-reduce.30 = (f32[4,32,64]{2,1,0:T(8,128)S(1)}, f32[3,16,32]{2,1,0:T(8,128)S(1)}, f32[32,16]{0,1:T(8,128)S(1)}, f32[7,32]{1,0:T(8,128)S(1)}) all-reduce(f32[4,32,64]{2,1,0:T(8,128)S(1)} %get-tuple-element.5, f32[3,16,32]{2,1,0:T(8,128)S(1)} %get-tuple-element.6, ...), channel_id=1, replica_groups=mesh['dp'=4,'tm'=8] {'dp'}, use_global_device_ids=true, to_apply=%region_5.6 | all-reduce | flops 10464 | bytes 83712 | tf_op jit(solution)/shard_map/psum | solution.py:256
  (142 shorter events, 31.0 us)
Async XLA Ops:
  0.6 30.6 %copy-start = (f32[32,16]{0,1:T(8,128)S(1)}, f32[32,16]{0,1:T(8,128)}, u32[]{:S(2)}) copy-start(f32[32,16]{0,1:T(8,128)} %param.11) | copy-start | bytes 6148
  1.9 41.5 %collective-permute-start.3 = (f32[1,768]{1,0:T(1,128)}, f32[1,768]{1,0:T(1,128)}, u32[]{:S(2)}, u32[]{:S(2)}) collective-permute-start(f32[1,768]{1,0:T(1,128)} %slice.296), channel_id=1, source_target_pairs={{1,0},{2,1},{3,2},{4,3},{5,4},{6,5},{7,6},{9,8},{10,9},{11,10},{12... | collective-permute-start | bytes 9224 | tf_op jit(solution)/shard_map/ppermute | solution.py:32
  4.1 20.5 %collective-permute-start = (f32[1,64,4]{2,1,0:T(8,128)S(1)}, f32[1,64,4]{2,1,0:T(8,128)S(1)}, u32[]{:S(2)}, u32[]{:S(2)}) collective-permute-start(f32[1,64,4]{2,1,0:T(8,128)S(1)} %get-tuple-element.19), channel_id=1, source_target_pairs={{0,1},{1,2},{2,3},{3,4},{4,5},{5,6},{6,7},{8,9},{9,10},{10,11},{11... | collective-permute-start | bytes 3080 | tf_op jit(solution)/shard_map/ppermute | solution.py:20
  9.6 15.0 %collective-permute-start.1 = (f32[1,64,4]{2,1,0:T(8,128)S(1)}, f32[1,64,4]{2,1,0:T(8,128)S(1)}, u32[]{:S(2)}, u32[]{:S(2)}) collective-permute-start(f32[1,64,4]{2,1,0:T(8,128)S(1)} %get-tuple-element.20), channel_id=1, source_target_pairs={{1,0},{2,1},{3,2},{4,3},{5,4},{6,5},{7,6},{9,8},{10,9},{11,10},{12... | collective-permute-start | bytes 3080 | tf_op jit(solution)/shard_map/ppermute | solution.py:22
  15.1 9.5 %copy-start.7 = (f32[1,64,512]{2,1,0:T(8,128)S(1)}, f32[1,64,512]{2,1,0:T(8,128)}, u32[]{:S(2)}) copy-start(f32[1,64,512]{2,1,0:T(8,128)} %param.7) | copy-start | bytes 393220
  15.1 9.5 %copy-start.11 = (f32[4,32,64]{2,1,0:T(8,128)S(1)}, f32[4,32,64]{2,1,0:T(8,128)}, u32[]{:S(2)}) copy-start(f32[4,32,64]{2,1,0:T(8,128)} %param.9) | copy-start | bytes 98308
  24.6 2.0 %copy-start.17 = (f32[1,64,4]{2,1,0:T(8,128)}, f32[1,64,4]{2,1,0:T(8,128)S(1)}, u32[]{:S(2)}) copy-start(f32[1,64,4]{2,1,0:T(8,128)S(1)} %collective-permute-done) | copy-start | bytes 3076
  24.6 1.9 %copy-start.19 = (f32[1,64,4]{2,1,0:T(8,128)}, f32[1,64,4]{2,1,0:T(8,128)S(1)}, u32[]{:S(2)}) copy-start(f32[1,64,4]{2,1,0:T(8,128)S(1)} %collective-permute-done.1) | copy-start | bytes 3076
  25.2 1.1 copy-start.4
  27.9 2.4 %copy-start.6 = (f32[1,32,1040]{2,1,0:T(8,128)}, f32[1,32,1040]{2,1,0:T(8,128)S(1)}, u32[]{:S(2)}) copy-start(f32[1,32,1040]{2,1,0:T(8,128)S(1)} %copy.17) | copy-start | bytes 399364
  32.6 5.9 %copy-start.9 = (f32[1,32,1040]{2,1,0:T(8,128)}, f32[1,32,1040]{2,1,0:T(8,128)S(1)}, u32[]{:S(2)}) copy-start(f32[1,32,1040]{2,1,0:T(8,128)S(1)} %get-tuple-element.78) | copy-start | bytes 399364
  39.5 2.0 %copy-start.14 = (f32[1,1040]{1,0:T(1,128)}, f32[1,1040]{1,0:T(1,128)S(1)}, u32[]{:S(2)}) copy-start(f32[1,1040]{1,0:T(1,128)S(1)} %squeeze.11) | copy-start | bytes 12484
  42.1 14.1 %collective-permute-start.2 = (f32[1,768]{1,0:T(1,128)}, f32[1,768]{1,0:T(1,128)}, u32[]{:S(2)}, u32[]{:S(2)}) collective-permute-start(f32[1,768]{1,0:T(1,128)} %slice.333), channel_id=1, source_target_pairs={{1,0},{2,1},{3,2},{4,3},{5,4},{6,5},{7,6},{9,8},{10,9},{11,10},{12... | collective-permute-start | bytes 9224 | tf_op jit(solution)/shard_map/ppermute | solution.py:32
  44.1 0.6 copy-start.15
  51.0 4.3 %copy-start.2 = (f32[256,128]{1,0:T(8,128)S(1)}, f32[256,128]{1,0:T(8,128)}, u32[]{:S(2)}) copy-start(f32[256,128]{1,0:T(8,128)} %get-tuple-element.79) | copy-start | bytes 393220
  51.0 4.3 %copy-start.3 = (f32[256,128]{1,0:T(8,128)S(1)}, f32[256,128]{1,0:T(8,128)}, u32[]{:S(2)}) copy-start(f32[256,128]{1,0:T(8,128)} %get-tuple-element.80) | copy-start | bytes 393220
  51.0 5.2 %copy-start.16 = (f32[1,1024]{1,0:T(1,128)S(1)}, f32[1,1024]{1,0:T(1,128)}, u32[]{:S(2)}) copy-start(f32[1,1024]{1,0:T(1,128)} %get-tuple-element.57) | copy-start | bytes 12292
  71.6 20.2 %collective-permute-start.5 = (f32[1,768]{1,0:T(1,128)S(1)}, f32[1,768]{1,0:T(1,128)S(1)}, u32[]{:S(2)}, u32[]{:S(2)}) collective-permute-start(f32[1,768]{1,0:T(1,128)S(1)} %pad.112), channel_id=1, source_target_pairs={{0,1},{1,2},{2,3},{3,4},{4,5},{5,6},{6,7},{8,9},{9,10},{10,11},{11... | collective-permute-start | bytes 9224 | tf_op jit(solution)/shard_map/ppermute | solution.py:32
  77.8 3.7 %copy-start.23 = (f32[64]{0:T(128)S(1)}, f32[64]{0:T(128)}, u32[]{:S(2)}) copy-start(f32[64]{0:T(128)} %get-tuple-element.71) | copy-start | bytes 772
  77.9 3.7 %copy-start.24 = (f32[64]{0:T(128)S(1)}, f32[64]{0:T(128)}, u32[]{:S(2)}) copy-start(f32[64]{0:T(128)} %get-tuple-element.72) | copy-start | bytes 772
  77.9 4.1 %copy-start.22 = (f32[1,4,1024]{2,1,0:T(4,128)S(1)}, f32[1,4,1024]{2,1,0:T(4,128)}, u32[]{:S(2)}) copy-start(f32[1,4,1024]{2,1,0:T(4,128)} %fusion.15) | copy-start | bytes 49156
  81.6 1.6 copy-start.1
  83.2 8.6 %copy-start.21 = (f32[1,1216]{1,0:T(1,128)S(1)}, f32[1,1216]{1,0:T(1,128)}, u32[]{:S(2)}) copy-start(f32[1,1216]{1,0:T(1,128)} %reshape.974) | copy-start | bytes 14596
  86.7 43.6 %copy-start.10 = (f32[1,32,1040]{2,1,0:T(8,128)S(1)}, f32[1,32,1040]{2,1,0:T(8,128)}, u32[]{:S(2)}) copy-start(f32[1,32,1040]{2,1,0:T(8,128)} %copy-done.9) | copy-start | bytes 399364
  86.8 6.3 %collective-permute-start.4 = (f32[1,768]{1,0:T(1,128)S(1)}, f32[1,768]{1,0:T(1,128)S(1)}, u32[]{:S(2)}, u32[]{:S(2)}) collective-permute-start(f32[1,768]{1,0:T(1,128)S(1)} %slice.347), channel_id=1, source_target_pairs={{0,1},{1,2},{2,3},{3,4},{4,5},{5,6},{6,7},{8,9},{9,10},{10,11},{11... | collective-permute-start | bytes 9224 | tf_op jit(solution)/shard_map/ppermute | solution.py:32
  121.9 5.8 %collective-permute-start.7 = (f32[1,1,8]{2,1,0:T(1,128)S(1)}, f32[1,1,8]{2,1,0:T(1,128)S(1)}, u32[]{:S(2)}, u32[]{:S(2)}) collective-permute-start(f32[1,1,8]{2,1,0:T(1,128)S(1)} %get-tuple-element.65), channel_id=1, source_target_pairs={{1,0},{2,1},{3,2},{4,3},{5,4},{6,5},{7,6},{9,8},{10,9},{11,10},{12... | collective-permute-start | bytes 104 | tf_op jit(solution)/shard_map/ppermute | solution.py:22
  123.2 5.8 %collective-permute-start.6 = (f32[1,1,8]{2,1,0:T(1,128)S(1)}, f32[1,1,8]{2,1,0:T(1,128)S(1)}, u32[]{:S(2)}, u32[]{:S(2)}) collective-permute-start(f32[1,1,8]{2,1,0:T(1,128)S(1)} %get-tuple-element.66), channel_id=1, source_target_pairs={{0,1},{1,2},{2,3},{3,4},{4,5},{5,6},{6,7},{8,9},{9,10},{10,11},{11... | collective-permute-start | bytes 104 | tf_op jit(solution)/shard_map/ppermute | solution.py:20
  129.1 3.1 %copy-start.13 = (f32[3,16,32]{2,1,0:T(8,128)S(1)}, f32[3,16,32]{2,1,0:T(8,128)}, u32[]{:S(2)}) copy-start(f32[3,16,32]{2,1,0:T(8,128)} %param.10) | copy-start | bytes 18436
  131.1 2.8 %copy-start.5 = (f32[1,64,519]{2,1,0:T(8,128)S(1)}, f32[1,64,519]{2,1,0:T(8,128)}, u32[]{:S(2)}) copy-start(f32[1,64,519]{2,1,0:T(8,128)} %copy-done.4) | copy-start | bytes 398596
  131.5 2.7 %copy-start.8 = (f32[1,64,512]{2,1,0:T(8,128)S(1)}, f32[1,64,512]{2,1,0:T(8,128)}, u32[]{:S(2)}) copy-start(f32[1,64,512]{2,1,0:T(8,128)} %param.7) | copy-start | bytes 393220
  131.5 2.7 %copy-start.18 = (f32[1,64,4]{2,1,0:T(8,128)S(1)}, f32[1,64,4]{2,1,0:T(8,128)}, u32[]{:S(2)}) copy-start(f32[1,64,4]{2,1,0:T(8,128)} %copy-done.17) | copy-start | bytes 3076
  131.5 2.7 %copy-start.20 = (f32[1,64,4]{2,1,0:T(8,128)S(1)}, f32[1,64,4]{2,1,0:T(8,128)}, u32[]{:S(2)}) copy-start(f32[1,64,4]{2,1,0:T(8,128)} %copy-done.19) | copy-start | bytes 3076
  133.8 58.6 %copy-start.12 = (f32[4,32,64]{2,1,0:T(8,128)S(1)}, f32[4,32,64]{2,1,0:T(8,128)}, u32[]{:S(2)}) copy-start(f32[4,32,64]{2,1,0:T(8,128)} %param.9) | copy-start | bytes 98308
